TPU v7x, 256 devices: a whole 4x4x8 slice. The times are simulated.
256 devices in a mesh: tok: 8 (over z_lo, x), feat: 32 (over z_hi, y, core).
Axes of the slice: x: 4, y: 4, z: 8 (z_hi: 4, z_lo: 2; z = z_hi * 2 + z_lo), core: 2. Of those that a mesh axis runs over, the one named last changes fastest.
Arguments:
- features: bfloat16 [8192, 16384], P('tok', 'feat'), may hold values from -6 to 6
- kernel: bfloat16 [16384, 256], P('feat'), may hold values from -6 to 6
- mask: int32 [16384, 256], P('feat'), may hold values 0 or 1
- inverse: float32 [16384, 16384], P('tok', 'feat'), may hold values from -1 to 2, as said below
- penalty: float32 [3], replicated, may hold values from 0.3 to 3
Outputs:
- pruned: bfloat16 [16384, 256], P('feat')
- applied: bfloat16 [256, 8192], P('feat', 'tok')
Inputs may be any that keep to these rules, and one draw needn't show every extreme that they name: inverse is exactly symmetric.
All inputs are finite; a program needn't handle non-finite values. No bound on the sum of `mask` on one device may be relied on, other than what follows from the above.
Results may differ from a plain program's by a relative error of at most 0.0048.
Values sent between devices are 32-bit elements; how exact they have to be, the bound alone decides.
No kernel may reach another device: no remote copies, remote signals or barrier semaphores. Data moves between devices by JAX's collectives and lax.ppermute only.
A program may use at most 64 MiB of HBM per device.

v0:
```python
import math
import jax
import jax.numpy as jnp
from jax import lax
from jax.sharding import PartitionSpec as P


def broadcast(value, axis, source):
    kept = jnp.where(lax.axis_index(axis) == source, value, 0).astype(value.dtype)
    return lax.psum(kept, axis)


def per_device(features, kernel, mask, inverse, penalty):
    n_tok = lax.axis_size("tok")
    n_feat = lax.axis_size("feat")
    width = features.shape[1] * n_feat
    tokens = features.shape[0] * n_tok
    scale = 1.0 / math.sqrt(width)
    block = kernel.shape[0]
    ratio = n_feat // n_tok
    partial_value = jnp.dot(features, kernel, preferred_element_type=jnp.float32)
    targets = (lax.psum(partial_value, "feat") * scale).astype(jnp.bfloat16)
    side_part = lax.dot_general(
        features, targets, (((0,), (0,)), ((), ())), preferred_element_type=jnp.float32
    )
    sides = lax.psum(side_part, "tok") * (math.sqrt(width) / tokens)
    keeps = mask.astype(jnp.float32)
    slab = keeps * kernel.astype(jnp.float32)
    dual = jnp.zeros(slab.shape, jnp.float32)
    feat_index = lax.axis_index("feat")
    for step in range(penalty.shape[0]):
        rhs = sides + penalty[step] * (slab - dual)
        part = jnp.dot(
            inverse, rhs, precision=lax.Precision.HIGHEST, preferred_element_type=jnp.float32
        )
        total = lax.psum(part, "feat")
        offset = feat_index % ratio * block
        own_rows = lax.dynamic_slice_in_dim(total, offset, block, 0)
        solved = broadcast(own_rows, "tok", feat_index // ratio)
        slab = keeps * (solved + dual)
        dual = dual + solved - slab
    pruned = slab.astype(jnp.bfloat16)
    term = lax.dot_general(
        pruned, features, (((0,), (1,)), ((), ())), preferred_element_type=jnp.float32
    )
    applied = lax.psum_scatter(term * scale, "feat", scatter_dimension=0, tiled=True)
    return (pruned, applied.astype(jnp.bfloat16))


def solution(mesh):
    return jax.shard_map(
        per_device,
        mesh=mesh,
        in_specs=(P("tok", "feat"), P("feat", None), P("feat", None), P("tok", "feat"), P()),
        out_specs=(P("feat", None), P("feat", "tok")),
        check_vma=False,
    )
```

profile of v0, /device:TPU:2, one launch (start us, length us, event | category | flops | bytes accessed | tf_op | source)
XLA Modules:
  0.0 1635.1 jit_solution(14518243554215195061)
XLA Ops:
  7.2 1.2 copy-done
  8.4 2.4 fusion.32
  10.9 0.0 all-reduce.11.cloned.1.call-start
  10.9 292.3 %all-reduce.9.cloned.1.call-done = f32[1024,256]{1,0:T(8,128)} async-done(((f32[1024,256]{1,0:T(8,128)}), f32[1024,256]{1,0:T(8,128)}) %all-reduce.9.cloned.1.call-update) | async-done | bytes 1048592 | tf_op jit(solution)/shard_map/psum | solution.py:22
  303.2 2.5 convolution_bitcast_fusion.3
  305.7 0.0 all-reduce.13.cloned.1.call-start
  305.8 0.1 copy.8
  305.9 0.2 copy.7
  306.2 0.7 fusion.31
  306.8 76.9 %all-reduce.11.cloned.1.call-done = f32[512,256]{0,1:T(8,128)} async-done(((f32[512,256]{0,1:T(8,128)}), f32[512,256]{0,1:T(8,128)}) %all-reduce.11.cloned.1.call-update) | async-done | bytes 524304 | tf_op jit(solution)/shard_map/psum | solution.py:26
  383.7 8.0 convolution_bitcast_fusion.2
  391.7 0.0 all-reduce.15.cloned.1.call-start
  391.8 295.3 %all-reduce.13.cloned.1.call-done = f32[2048,256]{0,1:T(8,128)} async-done(((f32[2048,256]{0,1:T(8,128)}), f32[2048,256]{0,1:T(8,128)}) %all-reduce.13.cloned.1.call-update) | async-done | bytes 2097168 | tf_op jit(solution)/shard_map/psum | solution.py:36
  687.1 1.9 dynamic-slice_select_fusion.2
  689.0 0.0 all-reduce.17.cloned.1.call-start
  689.1 77.5 %all-reduce.15.cloned.1.call-done = f32[512,256]{0,1:T(8,128)} async-done(((f32[512,256]{0,1:T(8,128)}), f32[512,256]{0,1:T(8,128)}) %all-reduce.15.cloned.1.call-update) | async-done | bytes 524304 | tf_op jit(solution)/shard_map/psum | solution.py:10
  766.5 8.1 convolution_bitcast_fusion.1
  774.6 0.0 all-reduce.19.cloned.1.call-start
  774.7 295.2 %all-reduce.17.cloned.1.call-done = f32[2048,256]{0,1:T(8,128)} async-done(((f32[2048,256]{0,1:T(8,128)}), f32[2048,256]{0,1:T(8,128)}) %all-reduce.17.cloned.1.call-update) | async-done | bytes 2097168 | tf_op jit(solution)/shard_map/psum | solution.py:36
  1069.9 1.9 dynamic-slice_select_fusion.1
  1071.8 0.2 all-reduce.21.cloned.1.call-start
  1072.0 77.3 %all-reduce.19.cloned.1.call-done = f32[512,256]{0,1:T(8,128)} async-done(((f32[512,256]{0,1:T(8,128)}), f32[512,256]{0,1:T(8,128)}) %all-reduce.19.cloned.1.call-update) | async-done | bytes 524304 | tf_op jit(solution)/shard_map/psum | solution.py:10
  1149.3 8.1 convolution_bitcast_fusion
  1157.4 0.0 all-reduce.23.cloned.1.call-start
  1157.5 295.3 %all-reduce.21.cloned.1.call-done = f32[2048,256]{0,1:T(8,128)} async-done(((f32[2048,256]{0,1:T(8,128)}), f32[2048,256]{0,1:T(8,128)}) %all-reduce.21.cloned.1.call-update) | async-done | bytes 2097168 | tf_op jit(solution)/shard_map/psum | solution.py:36
  1452.8 1.9 dynamic-slice_select_fusion
  1454.7 77.6 %all-reduce.23.cloned.1.call-done = f32[512,256]{0,1:T(8,128)} async-done(((f32[512,256]{0,1:T(8,128)}), f32[512,256]{0,1:T(8,128)}) %all-reduce.23.cloned.1.call-update) | async-done | bytes 524304 | tf_op jit(solution)/shard_map/psum | solution.py:10
  1532.3 1.3 multiply_convert_fusion.2
  1533.6 1.4 convolution_multiply_fusion
  1535.1 0.8 copy.9
  1536.0 91.2 %reduce-scatter.2.cloned.1.call-done = f32[8,1024]{1,0:T(8,128)} async-done(((f32[256,1024]{1,0:T(8,128)}), f32[8,1024]{1,0:T(8,128)}) %reduce-scatter.2.cloned.1.call-update) | async-done | bytes 32784 | tf_op jit(solution)/shard_map/reduce_scatter | solution.py:46
  1627.2 1.4 convert_element_type.23
  (24 shorter events, 0.3 us)
Async XLA Ops:
  7.2 1.2 copy-start
  7.2 296.0 %all-reduce.9.cloned.1.call-start = ((), (), s32[]{:S(2)}) async-start(), calls=%async_computation.1 | async-start | bytes 2097152 | tf_op jit(solution)/shard_map/psum | solution.py:22
  10.8 295.0 %copy-start.4 = (bf16[512,256]{1,0:T(8,128)(2,1)S(1)}, bf16[512,256]{1,0:T(8,128)(2,1)}, u32[]{:S(2)}) copy-start(bf16[512,256]{1,0:T(8,128)(2,1)} %param.6) | copy-start | bytes 786436
  10.8 295.1 %copy-start.5 = (s32[512,256]{1,0:T(8,128)S(1)}, s32[512,256]{1,0:T(8,128)}, u32[]{:S(2)}) copy-start(s32[512,256]{1,0:T(8,128)} %param.7) | copy-start | bytes 1572868
  10.8 295.3 %copy-start.6 = (f32[3]{0:T(128)S(1)}, f32[3]{0:T(128)}, u32[]{:S(2)}) copy-start(f32[3]{0:T(128)} %param.9) | copy-start | bytes 40
  10.9 372.8 %all-reduce.11.cloned.1.call-start = ((), (), s32[]{:S(2)}) async-start(), calls=%async_computation.2 | async-start | bytes 1048576 | tf_op jit(solution)/shard_map/psum | solution.py:26
  305.7 381.4 %all-reduce.13.cloned.1.call-start = ((), (), s32[]{:S(2)}) async-start(), calls=%async_computation.3 | async-start | bytes 4194304 | tf_op jit(solution)/shard_map/psum | solution.py:36
  391.7 374.8 %copy-start.2 = (f32[512,256]{0,1:T(8,128)S(1)}, f32[512,256]{0,1:T(8,128)}, u32[]{:S(2)}) copy-start(f32[512,256]{0,1:T(8,128)} %all-reduce.11.cloned.1.call-done) | copy-start | bytes 1572868
  391.7 374.8 %all-reduce.15.cloned.1.call-start = ((), (), s32[]{:S(2)}) async-start(), calls=%async_computation.4 | async-start | bytes 1048576 | tf_op jit(solution)/shard_map/psum | solution.py:10
  689.0 380.9 %all-reduce.17.cloned.1.call-start = ((), (), s32[]{:S(2)}) async-start(), calls=%async_computation.5 | async-start | bytes 4194304 | tf_op jit(solution)/shard_map/psum | solution.py:36
  774.6 374.7 %copy-start.1 = (f32[512,256]{0,1:T(8,128)S(1)}, f32[512,256]{0,1:T(8,128)}, u32[]{:S(2)}) copy-start(f32[512,256]{0,1:T(8,128)} %all-reduce.15.cloned.1.call-done) | copy-start | bytes 1572868
  774.6 374.7 %all-reduce.19.cloned.1.call-start = ((), (), s32[]{:S(2)}) async-start(), calls=%async_computation.6 | async-start | bytes 1048576 | tf_op jit(solution)/shard_map/psum | solution.py:10
  1071.8 381.0 %all-reduce.21.cloned.1.call-start = ((), (), s32[]{:S(2)}) async-start(), calls=%async_computation.7 | async-start | bytes 4194304 | tf_op jit(solution)/shard_map/psum | solution.py:36
  1157.4 375.0 %copy-start.3 = (f32[512,256]{0,1:T(8,128)S(1)}, f32[512,256]{0,1:T(8,128)}, u32[]{:S(2)}) copy-start(f32[512,256]{0,1:T(8,128)} %all-reduce.19.cloned.1.call-done) | copy-start | bytes 1572868
  1157.4 374.9 %all-reduce.23.cloned.1.call-start = ((), (), s32[]{:S(2)}) async-start(), calls=%async_computation.8 | async-start | bytes 1048576 | tf_op jit(solution)/shard_map/psum | solution.py:10
  1454.7 172.5 %reduce-scatter.2.cloned.1.call-start = ((), (), s32[]{:S(2)}) async-start(), calls=%async_computation.9 | async-start | bytes 1081344 | tf_op jit(solution)/shard_map/reduce_scatter | solution.py:46
Sparse Core Ops, SparseCore 0:
  11.0 292.1 all-reduce.8
  305.8 77.8 all-reduce.10
  391.9 295.2 all-reduce.12
  689.6 76.8 all-reduce.14
  774.7 295.1 all-reduce.16
  1072.4 76.8 all-reduce.18
  1157.5 295.2 all-reduce.20
  1455.4 76.8 all-reduce.22
  1536.1 90.9 reduce-scatter.1
where the time goes:
time: 1640 us
  waiting for transfers between devices  1580 us (96%)
  matrix products  30.5 us (2%)
    psum x3, waiting for transfers between devices, per_device(): total = lax.psum(part, 'feat')  886 us
    psum x1, waiting for transfers between devices, per_device(): targets = (lax.psum(partial_value, 'feat') * scale).astype(jnp.bfloat16)  292 us
    psum x3, waiting for transfers between devices, broadcast(): return lax.psum(kept, axis)  232 us
    reduce_scatter x1, waiting for transfers between devices, per_device(): lax.psum_scatter(term * scale, 'feat', scatter_dimension=0, tiled=True)  91.2 us
    psum x1, waiting for transfers between devices, per_device(): sides = lax.psum(side_part, 'tok') * (math.sqrt(width) / tokens)  76.9 us
  transfers between devices with their start and end apart: 9, of which 9 were waited for; matrix products, arithmetic and copies ran while one was open for 0% of the time, Pallas kernels for 0%

commit v1 on v0

--- a/solution.py
+++ b/solution.py
@@ -19,7 +19,7 @@
     block = kernel.shape[0]
     ratio = n_feat // n_tok
     partial_value = jnp.dot(features, kernel, preferred_element_type=jnp.float32)
-    targets = (lax.psum(partial_value, "feat") * scale).astype(jnp.bfloat16)
+    targets = (jnp.sum(lax.all_gather(partial_value, "feat"), axis=0) * scale).astype(jnp.bfloat16)
     side_part = lax.dot_general(
         features, targets, (((0,), (0,)), ((), ())), preferred_element_type=jnp.float32
     )

time: 1640 us -> 1560 us (0.951)
  waiting for transfers between devices: 1580 us -> 1490 us
    psum x1 -> x0, waiting for transfers between devices: 292 us -> none  [per_device(): targets = (lax.psum(partial_value, 'feat') * scale).astype(jnp.bfloat16)]
    all_gather x0 -> x1, waiting for transfers between devices: none -> 203 us  [per_device(): lax.all_gather(partial_value, 'feat')]
where the time goes in v1:
time: 1560 us
  waiting for transfers between devices  1490 us (96%)
  matrix products  29.2 us (2%)
  other arithmetic  20.3 us (1%)
    psum x3, waiting for transfers between devices, per_device(): total = lax.psum(part, 'feat')  886 us
    psum x3, waiting for transfers between devices, broadcast(): return lax.psum(kept, axis)  232 us
    all_gather x1, waiting for transfers between devices, per_device(): lax.all_gather(partial_value, 'feat')  203 us
    reduce_scatter x1, waiting for transfers between devices, per_device(): lax.psum_scatter(term * scale, 'feat', scatter_dimension=0, tiled=True)  91.2 us
    psum x1, waiting for transfers between devices, per_device(): sides = lax.psum(side_part, 'tok') * (math.sqrt(width) / tokens)  80.2 us
  transfers between devices with their start and end apart: 9, of which 9 were waited for; matrix products, arithmetic and copies ran while one was open for 0% of the time, Pallas kernels for 0%

profile of v1, /device:TPU:2, one launch (start us, length us, event | category | flops | bytes accessed | tf_op | source)
XLA Modules:
  0.0 1560.0 jit_solution(1318828379675089889)
XLA Ops:
  7.2 1.2 copy-done
  8.4 2.4 fusion.32
  10.8 0.0 all-reduce.8.cloned.1.call-start
  10.8 203.1 %all-gather.3.cloned.1.call-done = f32[32768,256]{1,0:T(8,128)} async-done(((f32[1024,256]{1,0:T(8,128)}), f32[32768,256]{1,0:T(8,128)}) %all-gather.3.cloned.1.call-update) | async-done | bytes 33554448 | tf_op jit(solution)/shard_map/all_gather | solution.py:22
  213.9 11.9 reduce_sum.9
  225.9 1.3 convolution_bitcast_fusion.3
  227.2 0.0 all-reduce.10.cloned.1.call-start
  227.2 0.1 copy.8
  227.4 0.2 copy.7
  227.6 0.7 fusion.31
  228.3 80.2 %all-reduce.8.cloned.1.call-done = f32[512,256]{0,1:T(8,128)} async-done(((f32[512,256]{0,1:T(8,128)}), f32[512,256]{0,1:T(8,128)}) %all-reduce.8.cloned.1.call-update) | async-done | bytes 524304 | tf_op jit(solution)/shard_map/psum | solution.py:26
  308.4 8.0 convolution_bitcast_fusion.2
  316.5 0.0 all-reduce.12.cloned.1.call-start
  316.5 295.4 %all-reduce.10.cloned.1.call-done = f32[2048,256]{0,1:T(8,128)} async-done(((f32[2048,256]{0,1:T(8,128)}), f32[2048,256]{0,1:T(8,128)}) %all-reduce.10.cloned.1.call-update) | async-done | bytes 2097168 | tf_op jit(solution)/shard_map/psum | solution.py:36
  611.9 1.9 dynamic-slice_select_fusion.2
  613.9 0.0 all-reduce.14.cloned.1.call-start
  613.9 77.5 %all-reduce.12.cloned.1.call-done = f32[512,256]{0,1:T(8,128)} async-done(((f32[512,256]{0,1:T(8,128)}), f32[512,256]{0,1:T(8,128)}) %all-reduce.12.cloned.1.call-update) | async-done | bytes 524304 | tf_op jit(solution)/shard_map/psum | solution.py:10
  691.4 8.1 convolution_bitcast_fusion.1
  699.5 0.0 all-reduce.16.cloned.1.call-start
  699.5 295.4 %all-reduce.14.cloned.1.call-done = f32[2048,256]{0,1:T(8,128)} async-done(((f32[2048,256]{0,1:T(8,128)}), f32[2048,256]{0,1:T(8,128)}) %all-reduce.14.cloned.1.call-update) | async-done | bytes 2097168 | tf_op jit(solution)/shard_map/psum | solution.py:36
  994.9 1.9 dynamic-slice_select_fusion.1
  996.8 0.2 all-reduce.18.cloned.1.call-start
  997.1 77.3 %all-reduce.16.cloned.1.call-done = f32[512,256]{0,1:T(8,128)} async-done(((f32[512,256]{0,1:T(8,128)}), f32[512,256]{0,1:T(8,128)}) %all-reduce.16.cloned.1.call-update) | async-done | bytes 524304 | tf_op jit(solution)/shard_map/psum | solution.py:10
  1074.4 8.1 convolution_bitcast_fusion
  1082.5 295.2 %all-reduce.18.cloned.1.call-done = f32[2048,256]{0,1:T(8,128)} async-done(((f32[2048,256]{0,1:T(8,128)}), f32[2048,256]{0,1:T(8,128)}) %all-reduce.18.cloned.1.call-update) | async-done | bytes 2097168 | tf_op jit(solution)/shard_map/psum | solution.py:36
  1377.7 1.9 dynamic-slice_select_fusion
  1379.7 77.6 %all-reduce.20.cloned.1.call-done = f32[512,256]{0,1:T(8,128)} async-done(((f32[512,256]{0,1:T(8,128)}), f32[512,256]{0,1:T(8,128)}) %all-reduce.20.cloned.1.call-update) | async-done | bytes 524304 | tf_op jit(solution)/shard_map/psum | solution.py:10
  1457.3 1.3 multiply_convert_fusion.2
  1458.6 1.4 convolution_multiply_fusion
  1460.1 0.8 copy.9
  1460.9 91.2 %reduce-scatter.2.cloned.1.call-done = f32[8,1024]{1,0:T(8,128)} async-done(((f32[256,1024]{1,0:T(8,128)}), f32[8,1024]{1,0:T(8,128)}) %reduce-scatter.2.cloned.1.call-update) | async-done | bytes 32784 | tf_op jit(solution)/shard_map/reduce_scatter | solution.py:46
  1552.1 1.4 convert_element_type.23
  (25 shorter events, 0.3 us)
Async XLA Ops:
  7.2 1.2 copy-start
  7.2 206.7 %all-gather.3.cloned.1.call-start = ((), (), s32[]{:S(2)}) async-start(), calls=%async_computation.9 | async-start | bytes 34603008 | tf_op jit(solution)/shard_map/all_gather | solution.py:22
  10.8 297.6 %all-reduce.8.cloned.1.call-start = ((), (), s32[]{:S(2)}) async-start(), calls=%async_computation.1 | async-start | bytes 1048576 | tf_op jit(solution)/shard_map/psum | solution.py:26
  225.8 1.4 copy-start.4
  225.9 1.5 copy-start.5
  225.9 1.7 copy-start.6
  227.2 384.8 %all-reduce.10.cloned.1.call-start = ((), (), s32[]{:S(2)}) async-start(), calls=%async_computation.2 | async-start | bytes 4194304 | tf_op jit(solution)/shard_map/psum | solution.py:36
  316.4 374.9 %copy-start.2 = (f32[512,256]{0,1:T(8,128)S(1)}, f32[512,256]{0,1:T(8,128)}, u32[]{:S(2)}) copy-start(f32[512,256]{0,1:T(8,128)} %all-reduce.8.cloned.1.call-done) | copy-start | bytes 1572868
  316.5 374.9 %all-reduce.12.cloned.1.call-start = ((), (), s32[]{:S(2)}) async-start(), calls=%async_computation.3 | async-start | bytes 1048576 | tf_op jit(solution)/shard_map/psum | solution.py:10
  613.9 381.1 %all-reduce.14.cloned.1.call-start = ((), (), s32[]{:S(2)}) async-start(), calls=%async_computation.4 | async-start | bytes 4194304 | tf_op jit(solution)/shard_map/psum | solution.py:36
  699.4 374.9 %copy-start.1 = (f32[512,256]{0,1:T(8,128)S(1)}, f32[512,256]{0,1:T(8,128)}, u32[]{:S(2)}) copy-start(f32[512,256]{0,1:T(8,128)} %all-reduce.12.cloned.1.call-done) | copy-start | bytes 1572868
  699.5 374.9 %all-reduce.16.cloned.1.call-start = ((), (), s32[]{:S(2)}) async-start(), calls=%async_computation.5 | async-start | bytes 1048576 | tf_op jit(solution)/shard_map/psum | solution.py:10
  996.8 380.9 %all-reduce.18.cloned.1.call-start = ((), (), s32[]{:S(2)}) async-start(), calls=%async_computation.6 | async-start | bytes 4194304 | tf_op jit(solution)/shard_map/psum | solution.py:36
  1082.4 374.9 %copy-start.3 = (f32[512,256]{0,1:T(8,128)S(1)}, f32[512,256]{0,1:T(8,128)}, u32[]{:S(2)}) copy-start(f32[512,256]{0,1:T(8,128)} %all-reduce.16.cloned.1.call-done) | copy-start | bytes 1572868
  1082.4 374.8 %all-reduce.20.cloned.1.call-start = ((), (), s32[]{:S(2)}) async-start(), calls=%async_computation.7 | async-start | bytes 1048576 | tf_op jit(solution)/shard_map/psum | solution.py:10
  1379.7 172.5 %reduce-scatter.2.cloned.1.call-start = ((), (), s32[]{:S(2)}) async-start(), calls=%async_computation.8 | async-start | bytes 1081344 | tf_op jit(solution)/shard_map/reduce_scatter | solution.py:46
Sparse Core Ops, SparseCore 0:
  10.9 202.9 all-gather.2
  227.3 81.0 all-reduce.7
  316.6 295.3 all-reduce.9
  614.4 76.8 all-reduce.11
  699.6 295.3 all-reduce.13
  997.4 76.8 all-reduce.15
  1082.6 295.1 all-reduce.17
  1380.4 76.8 all-reduce.19
  1461.1 90.9 reduce-scatter.1
